TPU v7x, 512 devices: a whole 4x4x16 slice. The times are simulated.
512 devices in a mesh: dp: 2 (over x_lo), context: 64 (over z, x_hi, core), tensor: 4 (over y).
Axes of the slice: x: 4 (x_hi: 2, x_lo: 2; x = x_hi * 2 + x_lo), y: 4, z: 16, core: 2. Of those that a mesh axis runs over, the one named last changes fastest.
Arguments:
- streams: bfloat16 [32768, 3, 8192], P(('dp', 'context'), None, 'tensor'), parts along dimension 0, may hold values from -6 to 6
- short_filter: float32 [3, 3, 8192], P(None, None, 'tensor'), may hold values from -3 to 3
- decay_rate: float32 [8192, 16], P('tensor'), as said below
- residue: float32 [8192, 16], P('tensor'), may hold values from -0.26 to 0.26
- bias: float32 [8192], P('tensor'), may hold values from -4 to 4
Outputs:
- gated: bfloat16 [32768, 8192], P(('dp', 'context'), 'tensor'), parts along dimension 0
There are 2 independent parts, one for each index of `dp`. A program takes and returns all parts, laid end to end along the dimension named above; an argument that names none is the same for every part. Nothing has to cross between parts.
Inputs may be any that keep to these rules, and one draw needn't show every extreme that they name: `decay_rate`: positive.
All inputs are finite; a program needn't handle non-finite values.
Results may differ from a plain program's by a relative error of at most 0.0058.
Values may be sent and summed in bfloat16 or wider, within the bound.
A program may use at most 128 MiB of HBM per device.

v0:
```python
import jax
import jax.numpy as jnp
from jax import lax
from jax.sharding import PartitionSpec as P

HIGH = lax.Precision.HIGHEST


def passed_along(value, axis, by):
    peers = lax.axis_size(axis)
    pairs = [(i, i + by) for i in range(peers) if 0 <= i + by < peers]
    return lax.ppermute(value, axis, pairs)


def featurize(raw, rim_rows, weights):
    extended = jnp.concatenate([rim_rows, raw], axis=0)
    return weights[0] * raw + weights[1] * extended[1:-1] + weights[2] * extended[:-2]


def block_terms(signal, rate, residue):
    channels, block_count, block_len = signal.shape
    log_pole = -rate
    positions = jnp.arange(block_len, dtype=jnp.float32)
    filter_taps = jnp.sum(
        residue[:, None, :] * jnp.exp(positions[None, :, None] * log_pole[:, None, :]), axis=2
    )
    offsets = jnp.arange(block_len, dtype=jnp.int32)
    lag_table = offsets[:, None] - offsets[None, :]
    toeplitz = jnp.where(
        lag_table[None] >= 0, jnp.take(filter_taps, jnp.maximum(lag_table, 0), axis=1), 0.0
    )
    within = jnp.einsum("cab,cnb->cna", toeplitz, signal, precision=HIGH)
    end_pow = jnp.exp((block_len - 1.0 - positions)[None, :, None] * log_pole[:, None, :])
    end_states = jnp.einsum("cbm,cnb->cnm", end_pow, signal, precision=HIGH)
    block_order = jnp.arange(block_count, dtype=jnp.float32)
    block_gaps = block_order[:, None] - 1.0 - block_order[None, :]
    span_pow = jnp.exp(
        block_len * jnp.maximum(block_gaps, 0.0)[None, None] * log_pole[:, :, None, None]
    )
    span_pow = jnp.where(block_gaps[None, None] >= 0.0, span_pow, 0.0)
    entering = jnp.einsum("cmnk,ckm->cnm", span_pow, end_states, precision=HIGH)
    out_pow = residue[:, None, :] * jnp.exp((positions + 1.0)[None, :, None] * log_pole[:, None, :])
    carried = jnp.einsum("cam,cnm->cna", out_pow, entering, precision=HIGH)
    tail_pow = jnp.exp(
        block_len * (block_count - 1.0 - block_order)[None, :, None] * log_pole[:, None, :]
    )
    end_state = jnp.sum(tail_pow * end_states, axis=1)
    return (within + carried, end_state)


def body(streams, short_filter, decay_rate, residue, bias):
    channels = streams.shape[2]
    context_size = lax.axis_size("context")
    context_rank = lax.axis_index("context")
    rim_rows = passed_along(streams[-2:], "context", 1).astype(jnp.float32)
    query_feat = featurize(streams[:, 0].astype(jnp.float32), rim_rows[:, 0], short_filter[0])
    key_feat = featurize(streams[:, 1].astype(jnp.float32), rim_rows[:, 1], short_filter[1])
    value_feat = featurize(streams[:, 2].astype(jnp.float32), rim_rows[:, 2], short_filter[2])
    product_rows = (key_feat * value_feat).astype(jnp.bfloat16)
    chan_dev = channels // context_size
    key_value = lax.all_to_all(product_rows, "context", split_axis=1, concat_axis=0, tiled=True)
    seq_len = key_value.shape[0]
    block_len = 256
    rate_dev = lax.dynamic_slice_in_dim(decay_rate, context_rank * chan_dev, chan_dev, 0)
    residue_dev = lax.dynamic_slice_in_dim(residue, context_rank * chan_dev, chan_dev, 0)
    bias_dev = lax.dynamic_slice_in_dim(bias, context_rank * chan_dev, chan_dev, 0)
    widened = key_value.astype(jnp.float32)
    signal = widened.T.reshape(chan_dev, seq_len // block_len, block_len)
    convolved, end_state = block_terms(signal, rate_dev, residue_dev)
    convolved = convolved.reshape(chan_dev, seq_len).T
    mixed = (convolved + bias_dev * widened).astype(jnp.bfloat16)
    returned = lax.all_to_all(mixed, "context", split_axis=0, concat_axis=1, tiled=True)
    return (query_feat * returned.astype(jnp.float32)).astype(jnp.bfloat16)


def solution(mesh):
    in_specs = (
        P(("dp", "context"), None, "tensor"),
        P(None, None, "tensor"),
        P("tensor", None),
        P("tensor", None),
        P("tensor"),
    )
    out_specs = P(("dp", "context"), "tensor")
    return jax.shard_map(body, mesh=mesh, in_specs=in_specs, out_specs=out_specs, check_vma=False)
```

profile of v0, /device:TPU:30, one launch (start us, length us, event | category | flops | bytes accessed | tf_op | source)
XLA Modules:
  0.0 400.6 jit_solution(13454285596592211302)
XLA Ops:
  0.0 0.9 slice.90
  0.9 1.9 collective-permute-start
  2.9 2.1 fusion.52
  4.9 1.3 copy.47
  6.3 1.3 copy.48
  7.6 0.0 copy-start.1
  7.6 3.2 bitcast_convert_fusion
  10.8 0.0 copy-done.1
  10.8 0.1 fusion.53
  10.9 0.0 collective-permute-done
  10.9 1.6 copy.33
  12.5 1.6 convert_element_type.44
  14.1 0.0 copy-start
  14.1 1.2 slice_bitcast_fusion.1
  15.3 0.8 copy-done
  16.1 5.6 %fusion.21 = bf16[256,2048]{0,1:T(8,128)(2,1)} fusion(f32[2,2048]{0,1:T(8,128)S(1)} %get-tuple-element.9, f32[256,2048]{0,1:T(8,128)S(1)} %get-tuple-element.20, f32[2,2048]{0,1:T(8,128)S(1)} %get-tuple-element.8, f32[256,2048]{0,1:T(8,128)S(1)} %copy-done, f32[2048]{0:T(1024)S(1)} %bitcast.85, f32[2048]{0:T(1024)S(1)} %bitcast.86, f32[2048]{0:T(1024)S(1)} %bitcast.82, ...), kind=kLoop, calls=%fused_computation.28 | loop fusion | flops 8388608 | bytes 5324800 | tf_op jit(solution)/shard_map/convert_element_type | solution.py:59
  21.7 20.2 %all-to-all-start = ((bf16[256,64,32]{0,2,1:T(8,128)(2,1)}), bf16[256,64,32]{0,2,1:T(8,128)(2,1)S(1)}, u32[]{:S(2)}, u32[]{:S(2)}) async-start(bf16[256,64,32]{0,2,1:T(8,128)(2,1)} %bitcast.18), calls=%async_computation | async-start | bytes 2097152 | tf_op jit(solution)/shard_map/all_to_all | solution.py:61
  41.9 0.8 dynamic-slice_negate_fusion
  42.7 0.1 copy.38
  42.8 0.1 copy.37
  42.9 0.2 multiply_reduce_fusion
  43.1 0.1 copy.39
  43.2 0.1 copy.52
  43.4 217.0 %gather_fusion = f32[65536,32]{1,0:T(8,128)} fusion(f32[32,256]{0,1:T(8,128)S(1)} %copy.39, s32[65536]{0:T(1024)S(1)} %broadcast_clamp_fusion), kind=kCustom, calls=%fused_computation | custom fusion | bytes 17039360 | tf_op jit(solution)/shard_map/jit(_take)/gather | solution.py:30
  260.5 22.2 %copy.40 = f32[256,256,32]{1,0,2:T(8,128)} copy(f32[256,256,32]{2,1,0:T(8,128)} %bitcast.65) | data formatting | bytes 16777216 | tf_op jit(solution)/shard_map/jit(_take)/gather | solution.py:30
  282.6 0.8 dynamic_slice.11
  283.4 0.1 maximum_compare_fusion
  283.5 0.1 fusion.48
  283.6 0.1 maximum_multiply_fusion
  283.6 0.0 all-to-all-done
  283.6 0.6 copy.51
  284.2 0.0 slice-start
  284.3 1.0 fusion.39
  285.3 0.0 slice-start.1
  285.3 27.1 %fusion = f32[32,16,1,64]{3,2,1,0:T(1,128)S(1)} fusion(f32[32,64,16,1]{1,3,2,0:T(1,128)S(1)} %bitcast.87, f32[32,16]{1,0:T(8,128)S(1)} %copy.38, f32[64,64]{1,0:T(8,128)S(1)} %maximum_multiply_fusion, pred[64,64]{1,0:T(8,128)(4,1)S(1)} %fusion.48), kind=kOutput, calls=%fused_computation.1 | convolution fusion | flops 29360128 | bytes 284672 | tf_op jit(solution)/shard_map/cmnk,ckm->cnm/dot_general | solution.py:41
  312.3 0.0 slice-done
  312.4 0.0 slice-done.1
  312.4 5.3 %fusion.4 = f32[32,64,256]{2,1,0:T(8,128)S(1)} fusion(bf16[32,64,256]{2,1,0:T(8,128)(2,1)S(1)} %bitcast.73, f32[256,256,32]{1,0,2:T(8,128)S(1)} %bitcast.67, pred[256,256]{1,0:T(8,128)(4,1)S(1)} %get-tuple-element.25, pred[256,256]{1,0:T(8,128)(4,1)S(1)} %get-tuple-element.24), kind=kOutput, calls=%fused_computation.5 | convolution fusion | flops 1614807040 | bytes 11665408 | tf_op jit(solution)/shard_map/cab,cnb->cna/dot_general | solution.py:32
  317.6 2.1 convolution_add_fusion
  319.7 1.2 copy.53
  321.0 0.1 copy.50
  321.0 0.3 fusion.35
  321.4 1.1 copy.56
  322.5 15.1 %all-to-all-start.1 = ((bf16[64,256,32]{1,2,0:T(8,128)(2,1)}), bf16[64,256,32]{1,2,0:T(8,128)(2,1)S(1)}, u32[]{:S(2)}, u32[]{:S(2)}) async-start(bf16[64,256,32]{1,2,0:T(8,128)(2,1)} %bitcast.64), calls=%async_computation.1 | async-start | bytes 2097152 | tf_op jit(solution)/shard_map/all_to_all | solution.py:72
  337.6 1.3 copy.46
  338.9 1.4 bitcast_convert_fusion.2
  340.3 53.4 %all-to-all-done.1 = bf16[64,256,32]{1,2,0:T(8,128)(2,1)S(1)} async-done(((bf16[64,256,32]{1,2,0:T(8,128)(2,1)}), bf16[64,256,32]{1,2,0:T(8,128)(2,1)S(1)}, u32[]{:S(2)}, u32[]{:S(2)}) %all-to-all-start.1) | async-done | bytes 1048608 | tf_op jit(solution)/shard_map/all_to_all | solution.py:72
  393.6 4.7 %fusion.31 = bf16[256,2048]{0,1:T(8,128)(2,1)} fusion(f32[2,2048]{0,1:T(8,128)} %get-tuple-element.10, f32[256,2048]{0,1:T(8,128)S(1)} %bitcast_convert_fusion.2, f32[2048]{0:T(1024)S(1)} %bitcast.78, f32[2048]{0:T(1024)S(1)} %bitcast.79, f32[2048]{0:T(1024)S(1)} %bitcast.80, bf16[64,256,32]{1,2,0:T(8,128)(2,1)S(1)} %all-to-all-done.1), kind=kLoop, calls=%fused_computation.38 | loop fusion | flops 5242880 | bytes 4235264 | tf_op jit(solution)/shard_map/convert_element_type | solution.py:73
  398.3 2.3 copy.43
  (6 shorter events, 0.1 us)
Async XLA Ops:
  0.9 9.9 %collective-permute-start = (bf16[2,3,2048]{2,0,1:T(2,128)(2,1)S(1)}, bf16[2,3,2048]{2,0,1:T(2,128)(2,1)S(1)}, u32[]{:S(2)}, u32[]{:S(2)}) collective-permute-start(bf16[2,3,2048]{2,0,1:T(2,128)(2,1)S(1)} %slice.90), channel_id=1, source_target_pairs={{0,4},{4,8},{8,12},{12,16},{16,20},{20,24},{24,28},{28,32},{32,36}... | collective-permute-start | bytes 73736 | tf_op jit(solution)/shard_map/ppermute | solution.py:12
  7.6 3.2 copy-start.1
  14.1 2.0 copy-start
  21.7 261.9 %all-to-all-start = ((bf16[256,64,32]{0,2,1:T(8,128)(2,1)}), bf16[256,64,32]{0,2,1:T(8,128)(2,1)S(1)}, u32[]{:S(2)}, u32[]{:S(2)}) async-start(bf16[256,64,32]{0,2,1:T(8,128)(2,1)} %bitcast.18), calls=%async_computation | async-start | bytes 2097152 | tf_op jit(solution)/shard_map/all_to_all | solution.py:61
  284.2 28.1 %slice-start = ((s8[8388608]{0:T(1024)(128)(4,1)}), s8[4194304]{0:T(1024)(128)(4,1)S(1)}, s32[]{:S(2)}) async-start(s8[8388608]{0:T(1024)(128)(4,1)} %bitcast.66), calls=%async_computation.2 | async-start | bytes 8388608
  285.3 27.1 %slice-start.1 = ((s8[8388608]{0:T(1024)(128)(4,1)}), s8[4194304]{0:T(1024)(128)(4,1)S(1)}, s32[]{:S(2)}) async-start(s8[8388608]{0:T(1024)(128)(4,1)} %bitcast.66), calls=%async_computation.3 | async-start | bytes 8388608
  322.5 71.2 %all-to-all-start.1 = ((bf16[64,256,32]{1,2,0:T(8,128)(2,1)}), bf16[64,256,32]{1,2,0:T(8,128)(2,1)S(1)}, u32[]{:S(2)}, u32[]{:S(2)}) async-start(bf16[64,256,32]{1,2,0:T(8,128)(2,1)} %bitcast.64), calls=%async_computation.1 | async-start | bytes 2097152 | tf_op jit(solution)/shard_map/all_to_all | solution.py:72
where the time goes:
time: 401 us
  local copies, waits for them, and re-layouts  256 us (64%)
  waiting for transfers between devices  53.4 us (13%)
  starting transfers between devices  37.2 us (9%)
  matrix products  35.4 us (9%)
  other arithmetic  18.2 us (5%)
    gather x2, local copies, waits for them, and re-layouts, block_terms(): jnp.take(filter_taps, jnp.maximum(lag_table, 0), axis=1)  239 us
    all_to_all x1, waiting for transfers between devices, body(): lax.all_to_all(mixed, 'context', split_axis=0, concat_axis=1, tiled=True)  53.4 us
    dot_general x1, matrix products, block_terms(): entering = jnp.einsum('cmnk,ckm->cnm', span_pow, end_states, precision=HIGH)  27.1 us
    all_to_all x1, starting transfers between devices, body(): lax.all_to_all(product_rows, 'context', split_axis=1, concat_axis=0, tile...  20.2 us
    all_to_all x1, starting transfers between devices, body(): lax.all_to_all(mixed, 'context', split_axis=0, concat_axis=1, tiled=True)  15.1 us
  transfers between devices with their start and end apart: 3, of which 1 were waited for; matrix products, arithmetic and copies ran while one was open for 63% of the time, Pallas kernels for 0%

commit v1 on v0

v1 whole, which is shorter than its diff:
```python
import functools

import jax
import jax.numpy as jnp
from jax import lax
from jax.experimental import pallas as pl
from jax.experimental.pallas import tpu as pltpu
from jax.sharding import PartitionSpec as P

F32 = jnp.float32
BF16 = jnp.bfloat16
MESH = pl.DeviceIdType.MESH
LANES = 128


def rows8():
    return lax.broadcasted_iota(jnp.int32, (8, LANES), 0)


def lag_tiles(tile, before):
    row = rows8()
    r1 = pltpu.roll(tile, 1, 0)
    r2 = pltpu.roll(tile, 2, 0)
    lag1 = jnp.where(row < 1, before[0], r1)
    lag2 = jnp.where(row < 2, before[1], r2)
    return lag1, lag2, (r1, r2)


def kernel(
    peers, tokens, groups, modes,
    x_hbm, w_hbm, rate_hbm, res_hbm, bias_hbm, out_hbm,
    w_ref, rate_ref, res_ref, bias_ref, xv, xt, kvt, yt, qf, ov, rate_cm, pole_cm, res_cm, ends, enter,
    rim_out, rim_in, send_c, got_c, scan_c, back_c,
    load_sem, out_sem, rim_sem, sem_a, sem_b,
):
    me = lax.axis_index("context")
    chunk = modes * groups // peers
    halves = groups // 8
    wide = 8 * LANES

    barrier = pltpu.get_barrier_semaphore()

    def greet(k, _):
        pl.semaphore_signal(
            barrier, inc=1, device_id={"context": lax.rem(me + k, peers)}, device_id_type=MESH
        )
        return 0

    tail = pltpu.make_async_copy(x_hbm.at[:, pl.ds(tokens - 16, 16), :], xt, load_sem.at[3])
    tail.start()
    loads = []
    for at, stream in enumerate((1, 2, 0)):
        load = pltpu.make_async_copy(x_hbm.at[stream], xv.at[stream], load_sem.at[at])
        load.start()
        loads.append(load)
    small = []
    pairs = ((rate_hbm, rate_ref), (res_hbm, res_ref), (w_hbm, w_ref), (bias_hbm, bias_ref))
    for at, (src, dst) in enumerate(pairs):
        load = pltpu.make_async_copy(src, dst, load_sem.at[4 + at])
        load.start()
        small.append(load)
    lax.fori_loop(1, peers, greet, 0)

    def prepare(g, _):
        lane = pl.ds(pl.multiple_of(g * LANES, LANES), LANES)
        rate = rate_ref[:, lane]
        where = pl.ds(g, modes, stride=groups)
        rate_cm[where, :] = rate
        pole_cm[where, :] = jnp.exp(-rate)
        res_cm[where, :] = res_ref[:, lane]
        return 0

    for load in small:
        load.wait()
    lax.fori_loop(0, groups, prepare, 0)

    tail.wait()
    wide_row = lax.broadcasted_iota(jnp.int32, (8, LANES * groups), 0)
    last = [xt[i, :, :].astype(F32)[8:16] for i in range(3)]
    rim_out[...] = jnp.where(
        wide_row < 2, pltpu.roll(last[0], 2, 0),
        jnp.where(wide_row < 4, pltpu.roll(last[1], 4, 0), pltpu.roll(last[2], 6, 0)),
    )

    def taps(i, lane):
        return [jnp.broadcast_to(w_ref[i, pl.ds(j, 1), lane], (8, LANES)) for j in range(3)]

    def products(h):
        def group(gi, _):
            g = h * 8 + gi
            lane = pl.ds(pl.multiple_of(g * LANES, LANES), LANES)
            wk, wv = taps(1, lane), taps(2, lane)
            zero = jnp.zeros((8, LANES), F32)
            kb, vb = (zero, zero), (zero, zero)
            for block in range(tokens // 16):
                k16 = xv[1, pl.ds(block * 16, 16), lane].astype(F32)
                v16 = xv[2, pl.ds(block * 16, 16), lane].astype(F32)
                for sub in range(2):
                    k, v = k16[sub * 8:sub * 8 + 8], v16[sub * 8:sub * 8 + 8]
                    k1, k2, kb = lag_tiles(k, kb)
                    v1, v2, vb = lag_tiles(v, vb)
                    kf = wk[0] * k + wk[1] * k1 + wk[2] * k2
                    vf = wv[0] * v + wv[1] * v1 + wv[2] * v2
                    kv = (kf * vf).astype(BF16).astype(F32)
                    if block == 0 and sub == 0:
                        kv = jnp.where(rows8() < 2, 0.0, kv)
                    at = (block * 16 + sub * 8) * groups + g
                    kvt[pl.ds(at, 8, stride=groups), :] = kv
            return 0

        lax.fori_loop(0, 8, group, 0)

    def vregs(ref, h):
        return [ref[pl.ds(m * groups + 8 * h, 8), :] for m in range(modes)]

    def token_rows(t, h):
        return pl.ds(pl.multiple_of(t * groups + 8 * h, 8), 8)

    def end_states(h):
        poles = vregs(pole_cm, h)

        def step(i, states):
            for j in range(8):
                x = kvt[token_rows(i * 8 + j, h), :]
                states = [s * p + x for s, p in zip(states, poles)]
            return states

        states = lax.fori_loop(0, tokens // 8, step, [jnp.zeros((8, LANES), F32)] * modes)
        for m in range(modes):
            ends[pl.ds(m * groups + 8 * h, 8), :] = states[m]

    loads[0].wait()
    loads[1].wait()
    products(0)
    end_states(0)

    pl.semaphore_wait(barrier, peers - 1)
    rim = pltpu.make_async_remote_copy(
        src_ref=rim_out, dst_ref=rim_in, send_sem=rim_sem.at[0], recv_sem=rim_sem.at[1],
        device_id={"context": lax.rem(me + 1, peers)}, device_id_type=MESH,
    )
    rim.start()
    for h in range(1, halves):
        products(h)
        end_states(h)
    loads[2].wait()
    rim.wait()

    def first_tile(g, _):
        lane = pl.ds(pl.multiple_of(g * LANES, LANES), LANES)
        edge = jnp.where(me > 0, rim_in[:, lane], 0.0)
        feats = []
        for i in range(3):
            w = taps(i, lane)
            x = xv[i, pl.ds(0, 16), lane].astype(F32)[0:8]
            before = (pltpu.roll(edge, (8 - 2 * i - 1) % 8, 0), pltpu.roll(edge, (8 - 2 * i) % 8, 0))
            x1, x2, _ = lag_tiles(x, before)
            feats.append(w[0] * x + w[1] * x1 + w[2] * x2)
        kvt[pl.ds(g, 8, stride=groups), :] = (feats[1] * feats[2]).astype(BF16).astype(F32)
        qf[pl.ds(0, 8), lane] = feats[0]
        return 0

    lax.fori_loop(0, groups, first_tile, 0)

    for h in range(halves):
        kv0 = kvt[pl.ds(8 * h, 8), :]
        kv1 = kvt[pl.ds(groups + 8 * h, 8), :]
        for m in range(modes):
            rows = pl.ds(m * groups + 8 * h, 8)
            far = jnp.exp(rate_cm[rows, :] * (2.0 - tokens))
            ends[rows, :] = ends[rows, :] + far * (pole_cm[rows, :] * kv0 + kv1)
    for o in range(peers):
        send_c[o, :, :] = ends[pl.ds(o * chunk, chunk), :]

    def ship(src, dst, sems):
        def one(k, _):
            peer = lax.rem(me + k, peers)
            pltpu.make_async_remote_copy(
                src_ref=src.at[peer], dst_ref=dst.at[me], send_sem=sems.at[0], recv_sem=sems.at[1],
                device_id={"context": peer}, device_id_type=MESH,
            ).start()
            return 0

        lax.fori_loop(1, peers, one, 0)

    def landed(ref, sem):
        part = ref.at[pl.ds(0, peers - 1)]
        pltpu.make_async_copy(part, part, sem).wait()

    ship(send_c, got_c, sem_a)
    got_c[pl.ds(me, 1), :, :] = send_c[pl.ds(me, 1), :, :]

    def local_part(h):
        poles, weights = vregs(pole_cm, h), vregs(res_cm, h)
        direct = bias_ref[pl.ds(8 * h, 8), :]

        def step(i, states):
            for j in range(4):
                rows = token_rows(i * 4 + j, h)
                x = kvt[rows, :]
                states = [s * p + x for s, p in zip(states, poles)]
                parts = [r * s for s, r in zip(states, weights)] + [direct * x]
                while len(parts) > 1:
                    parts = [a + b for a, b in zip(parts[::2], parts[1::2])] + (
                        [parts[-1]] if len(parts) % 2 else []
                    )
                yt[rows, :] = parts[0]
            return states

        lax.fori_loop(0, tokens // 4, step, [jnp.zeros((8, LANES), F32)] * modes)

    def query_part():
        def group(g, _):
            lane = pl.ds(pl.multiple_of(g * LANES, LANES), LANES)
            w = taps(0, lane)
            zero = jnp.zeros((8, LANES), F32)
            before = (zero, zero)
            for block in range(tokens // 16):
                x16 = xv[0, pl.ds(block * 16, 16), lane].astype(F32)
                for sub in range(2):
                    x = x16[sub * 8:sub * 8 + 8]
                    x1, x2, before = lag_tiles(x, before)
                    if block or sub:
                        qf[pl.ds(block * 16 + sub * 8, 8), lane] = w[0] * x + w[1] * x1 + w[2] * x2
            return 0

        lax.fori_loop(0, groups, group, 0)

    local_part(0)
    landed(got_c, sem_a.at[1])
    span = jnp.exp(rate_cm[pl.ds(me * chunk, chunk), :] * (-1.0 * tokens))

    def scan(i, state):
        for j in range(4):
            scan_c[pl.ds(i * 4 + j, 1), :, :] = state[None]
            state = state * span + got_c[i * 4 + j]
        return state

    lax.fori_loop(0, peers // 4, scan, jnp.zeros((chunk, LANES), F32))
    ship(scan_c, back_c, sem_b)
    back_c[pl.ds(me, 1), :, :] = scan_c[pl.ds(me, 1), :, :]
    for h in range(1, halves):
        local_part(h)
    query_part()
    landed(back_c, sem_b.at[1])
    for o in range(peers):
        enter[pl.ds(o * chunk, chunk), :] = back_c[o]

    outs = []
    for h in range(halves):
        poles = vregs(pole_cm, h)
        carried = [
            p * r * s for p, r, s in zip(poles, vregs(res_cm, h), vregs(enter, h))
        ]

        def step(i, terms, h=h, poles=poles):
            for j in range(8):
                rows = token_rows(i * 8 + j, h)
                parts = list(terms)
                while len(parts) > 1:
                    parts = [a + b for a, b in zip(parts[::2], parts[1::2])]
                yt[rows, :] = yt[rows, :] + parts[0]
                terms = [u * p for u, p in zip(terms, poles)]
            return terms

        lax.fori_loop(0, tokens // 8, step, carried)

        def gate(gi, _, h=h):
            g = h * 8 + gi
            lane = pl.ds(pl.multiple_of(g * LANES, LANES), LANES)
            for block in range(tokens // 16):
                at = block * 16
                mixed = jnp.concatenate(
                    [yt[pl.ds((at + sub) * groups + g, 8, stride=groups), :] for sub in (0, 8)], axis=0
                )
                mixed = mixed.astype(BF16).astype(F32)
                ov[pl.ds(at, 16), lane] = (qf[pl.ds(at, 16), lane] * mixed).astype(BF16)
            return 0

        lax.fori_loop(0, 8, gate, 0)
        cols = pl.ds(h * wide, wide)
        out = pltpu.make_async_copy(ov.at[:, cols], out_hbm.at[:, cols], out_sem.at[h])
        out.start()
        outs.append(out)
    landed(send_c, sem_a.at[0])
    landed(scan_c, sem_b.at[0])
    for out in outs:
        out.wait()


def body(streams, short_filter, decay_rate, residue, bias):
    tokens, _, channels = streams.shape
    modes = decay_rate.shape[1]
    groups = channels // LANES
    peers = lax.axis_size("context")
    chunk = modes * groups // peers
    args = (
        streams.transpose(1, 0, 2), short_filter, decay_rate.T, residue.T,
        bias.reshape(groups, LANES),
    )
    hbm = pl.BlockSpec(memory_space=pltpu.HBM)
    table = pltpu.VMEM((modes * groups, LANES), F32)
    chunks = pltpu.VMEM((peers, chunk, LANES), F32)
    return pl.pallas_call(
        functools.partial(kernel, peers, tokens, groups, modes),
        out_shape=jax.ShapeDtypeStruct((tokens, channels), BF16),
        in_specs=[hbm] * 5,
        out_specs=pl.BlockSpec(memory_space=pl.ANY),
        scratch_shapes=[
            pltpu.VMEM(short_filter.shape, F32),
            pltpu.VMEM((modes, channels), F32),
            pltpu.VMEM((modes, channels), F32),
            pltpu.VMEM((groups, LANES), F32),
            pltpu.VMEM((3, tokens, channels), BF16),
            pltpu.VMEM((3, 16, channels), BF16),
            pltpu.VMEM((tokens * groups, LANES), F32),
            pltpu.VMEM((tokens * groups, LANES), F32),
            pltpu.VMEM((tokens, channels), F32),
            pltpu.VMEM((tokens, channels), BF16),
            table, table, table, table, table,
            pltpu.VMEM((8, channels), F32),
            pltpu.VMEM((8, channels), F32),
            chunks, chunks, chunks, chunks,
            pltpu.SemaphoreType.DMA((8,)),
            pltpu.SemaphoreType.DMA((groups // 8,)),
            pltpu.SemaphoreType.DMA((2,)),
            pltpu.SemaphoreType.DMA((2,)),
            pltpu.SemaphoreType.DMA((2,)),
        ],
        compiler_params=pltpu.CompilerParams(
            collective_id=0, has_side_effects=True, vmem_limit_bytes=40 * 2**20
        ),
    )(*[pltpu.with_memory_space_constraint(a, pltpu.HBM) for a in args])


def solution(mesh):
    in_specs = (
        P(("dp", "context"), None, "tensor"),
        P(None, None, "tensor"),
        P("tensor", None),
        P("tensor", None),
        P("tensor"),
    )
    out_specs = P(("dp", "context"), "tensor")
    return jax.shard_map(body, mesh=mesh, in_specs=in_specs, out_specs=out_specs, check_vma=False)
```

time: 401 us -> 52.2 us (0.13)
  the two profiles are of different devices: /device:TPU:30 before, /device:TPU:1 now
where the time goes in v1:
time: 52.2 us; the launch traced here: 52.1 us
  Pallas kernels  51.1 us (98%)
  local copies, waits for them, and re-layouts  0.97 us (2%)
    pallas_call x1, Pallas kernels, body(): pl.pallas_call(functools.partial(kernel, peers, tokens, groups, modes), o...  51.1 us

profile of v1, /device:TPU:1, one launch (start us, length us, event | category | flops | bytes accessed | tf_op | source)
XLA Modules:
  0.0 52.1 jit_solution(16667881451471470102)
XLA Ops:
  0.0 51.1 %shard_map.55 = bf16[256,2048]{1,0:T(8,128)(2,1)S(1)} custom-call(bf16[3,256,2048]{2,1,0:T(8,128)(2,1)} %bitcast.4, f32[3,3,2048]{2,1,0:T(4,128)} %w_hbm.1, f32[16,2048]{1,0:T(8,128)} %bitcast.5, f32[16,2048]{1,0:T(8,128)} %bitcast.6, f32[16,128]{1,0:T(8,128)} %bitcast.7), custom_call_target="tpu_custom_call" | custom-call | tf_op jit(solution)/shard_map/pallas_call | solution.py:304
  51.1 1.0 %copy.7 = bf16[256,2048]{1,0:T(8,128)(2,1)} copy(bf16[256,2048]{1,0:T(8,128)(2,1)S(1)} %shard_map.55) | data formatting | bytes 2097152

commit v2 on v1

--- a/solution.py
+++ b/solution.py
@@ -30,20 +30,30 @@
     peers, tokens, groups, modes,
     x_hbm, w_hbm, rate_hbm, res_hbm, bias_hbm, out_hbm,
     w_ref, rate_ref, res_ref, bias_ref, xv, xt, kvt, yt, qf, ov, rate_cm, pole_cm, res_cm, ends, enter,
-    rim_out, rim_in, send_c, got_c, scan_c, back_c,
-    load_sem, out_sem, rim_sem, sem_a, sem_b,
+    rim_out, rim_in, got, total, totals, states_out,
+    load_sem, out_sem, rim_sem, got_sem, back_sem, total_send, total_recv, ready,
 ):
     me = lax.axis_index("context")
-    chunk = modes * groups // peers
+    team = modes
+    teams = peers // team
+    block, spot = me // team, lax.rem(me, team)
+    mine = pl.ds(pl.multiple_of(spot * groups, groups), groups)
     halves = groups // 8
     wide = 8 * LANES
 
+    def at_context(rank):
+        return {"device_id": {"context": rank}, "device_id_type": MESH}
+
+    def mate(step):
+        return block * team + lax.rem(spot + step, team)
+
     barrier = pltpu.get_barrier_semaphore()
 
-    def greet(k, _):
-        pl.semaphore_signal(
-            barrier, inc=1, device_id={"context": lax.rem(me + k, peers)}, device_id_type=MESH
-        )
+    def greet(rank):
+        pl.semaphore_signal(barrier, inc=1, **at_context(rank))
+
+    def greet_mate(step, _):
+        greet(mate(step))
         return 0
 
     tail = pltpu.make_async_copy(x_hbm.at[:, pl.ds(tokens - 16, 16), :], xt, load_sem.at[3])
@@ -59,7 +69,18 @@
         load = pltpu.make_async_copy(src, dst, load_sem.at[4 + at])
         load.start()
         small.append(load)
-    lax.fori_loop(1, peers, greet, 0)
+    lax.fori_loop(1, team, greet_mate, 0)
+    for step in range(1, teams):
+        @pl.when(block + step < teams)
+        def _(step=step):
+            greet(me + step * team)
+
+    @pl.when((spot == 0) & (block > 0))
+    def _():
+        greet(me - 1)
+
+    expected = team - 1 + block + jnp.where((spot == team - 1) & (block < teams - 1), 1, 0)
+
 
     def prepare(g, _):
         lane = pl.ds(pl.multiple_of(g * LANES, LANES), LANES)
@@ -134,21 +155,37 @@
     products(0)
     end_states(0)
 
-    pl.semaphore_wait(barrier, peers - 1)
+    pl.semaphore_wait(barrier, expected)
     rim = pltpu.make_async_remote_copy(
         src_ref=rim_out, dst_ref=rim_in, send_sem=rim_sem.at[0], recv_sem=rim_sem.at[1],
-        device_id={"context": lax.rem(me + 1, peers)}, device_id_type=MESH,
+        **at_context(lax.rem(me + 1, peers)),
     )
-    rim.start()
+
+    @pl.when(me < peers - 1)
+    def _():
+        rim.start()
+
+    for step in range(1, teams):
+        @pl.when(block >= step)
+        def _(step=step):
+            pl.semaphore_signal(ready.at[step - 1], inc=1, **at_context(me - step * team))
+
     for h in range(1, halves):
         products(h)
         end_states(h)
     loads[2].wait()
-    rim.wait()
+
+    @pl.when(me == 0)
+    def _():
+        rim_in[...] = jnp.zeros_like(rim_in)
+
+    @pl.when(me > 0)
+    def _():
+        rim.wait_recv()
 
     def first_tile(g, _):
         lane = pl.ds(pl.multiple_of(g * LANES, LANES), LANES)
-        edge = jnp.where(me > 0, rim_in[:, lane], 0.0)
+        edge = rim_in[:, lane]
         feats = []
         for i in range(3):
             w = taps(i, lane)
@@ -169,28 +206,38 @@
             rows = pl.ds(m * groups + 8 * h, 8)
             far = jnp.exp(rate_cm[rows, :] * (2.0 - tokens))
             ends[rows, :] = ends[rows, :] + far * (pole_cm[rows, :] * kv0 + kv1)
-    for o in range(peers):
-        send_c[o, :, :] = ends[pl.ds(o * chunk, chunk), :]
-
-    def ship(src, dst, sems):
-        def one(k, _):
-            peer = lax.rem(me + k, peers)
-            pltpu.make_async_remote_copy(
-                src_ref=src.at[peer], dst_ref=dst.at[me], send_sem=sems.at[0], recv_sem=sems.at[1],
-                device_id={"context": peer}, device_id_type=MESH,
-            ).start()
-            return 0
-
-        lax.fori_loop(1, peers, one, 0)
-
-    def landed(ref, sem):
-        part = ref.at[pl.ds(0, peers - 1)]
-        pltpu.make_async_copy(part, part, sem).wait()
-
-    ship(send_c, got_c, sem_a)
-    got_c[pl.ds(me, 1), :, :] = send_c[pl.ds(me, 1), :, :]
-
-    def local_part(h):
+    def rows_of(to):
+        return pl.ds(pl.multiple_of(to * groups, groups), groups)
+
+    def collect(step, _):
+        pltpu.make_async_remote_copy(
+            src_ref=ends.at[rows_of(lax.rem(spot + step, team))], dst_ref=got.at[spot],
+            send_sem=got_sem.at[0], recv_sem=got_sem.at[1], **at_context(mate(step)),
+        ).start()
+        return 0
+
+    lax.fori_loop(1, team, collect, 0)
+    got[pl.ds(spot, 1), :, :] = ends[mine, :][None]
+
+    def team_bytes(sem):
+        part = got.at[pl.ds(0, team - 1)]
+        return pltpu.make_async_copy(part, part, sem)
+
+    def forward(step):
+        return pltpu.make_async_remote_copy(
+            src_ref=total, dst_ref=totals.at[step - 1], send_sem=total_send.at[step - 1],
+            recv_sem=total_recv.at[step - 1], **at_context(lax.rem(me + step * team, peers)),
+        )
+
+    def push(step):
+        @pl.when(block + step < teams)
+        def _():
+            pl.semaphore_wait(ready.at[step - 1], 1)
+            forward(step).start()
+
+    blank = [jnp.zeros((8, LANES), F32)] * modes
+
+    def local_part(h, first, last, states):
         poles, weights = vregs(pole_cm, h), vregs(res_cm, h)
         direct = bias_ref[pl.ds(8 * h, 8), :]
 
@@ -207,7 +254,7 @@
                 yt[rows, :] = parts[0]
             return states
 
-        lax.fori_loop(0, tokens // 4, step, [jnp.zeros((8, LANES), F32)] * modes)
+        return lax.fori_loop(first // 4, last // 4, step, states)
 
     def query_part():
         def group(g, _):
@@ -226,25 +273,46 @@
 
         lax.fori_loop(0, groups, group, 0)
 
-    local_part(0)
-    landed(got_c, sem_a.at[1])
-    span = jnp.exp(rate_cm[pl.ds(me * chunk, chunk), :] * (-1.0 * tokens))
-
-    def scan(i, state):
-        for j in range(4):
-            scan_c[pl.ds(i * 4 + j, 1), :, :] = state[None]
-            state = state * span + got_c[i * 4 + j]
-        return state
-
-    lax.fori_loop(0, peers // 4, scan, jnp.zeros((chunk, LANES), F32))
-    ship(scan_c, back_c, sem_b)
-    back_c[pl.ds(me, 1), :, :] = scan_c[pl.ds(me, 1), :, :]
+    half = tokens // 2
+    kept = local_part(0, 0, half, blank)
+    kept = local_part(0, half, tokens, kept)
+    team_bytes(got_sem.at[1]).wait()
+    rate = rate_cm[mine, :]
+    span = jnp.exp(rate * (-1.0 * tokens))
+    leap = jnp.exp(rate * (-1.0 * tokens * team))
+    sums = got[0]
+    for j in range(1, team):
+        sums = sums * span + got[j]
+    total[...] = sums
+    push(1)
+    states_out[0, :, :] = jnp.zeros((groups, LANES), F32)
+    for step in range(teams - 1, 0, -1):
+        @pl.when(block >= step)
+        def _(step=step):
+            forward(step).wait_recv()
+            states_out[0, :, :] = states_out[0] * leap + totals[step - 1]
+
+    state = states_out[0]
+    for j in range(1, team):
+        state = state * span + got[j - 1]
+        states_out[j, :, :] = state
+
+    def give_back(step, _):
+        pltpu.make_async_remote_copy(
+            src_ref=states_out.at[lax.rem(spot + step, team)], dst_ref=enter.at[mine],
+            send_sem=back_sem.at[0], recv_sem=back_sem.at[1], **at_context(mate(step)),
+        ).start()
+        return 0
+
+    lax.fori_loop(1, team, give_back, 0)
+    enter[mine, :] = states_out[spot]
+    for step in range(2, teams):
+        push(step)
     for h in range(1, halves):
-        local_part(h)
+        kept = local_part(h, 0, half, blank)
+        kept = local_part(h, half, tokens, kept)
     query_part()
-    landed(back_c, sem_b.at[1])
-    for o in range(peers):
-        enter[pl.ds(o * chunk, chunk), :] = back_c[o]
+    team_bytes(back_sem.at[1]).wait()
 
     outs = []
     for h in range(halves):
@@ -282,8 +350,17 @@
         out = pltpu.make_async_copy(ov.at[:, cols], out_hbm.at[:, cols], out_sem.at[h])
         out.start()
         outs.append(out)
-    landed(send_c, sem_a.at[0])
-    landed(scan_c, sem_b.at[0])
+    @pl.when(me < peers - 1)
+    def _():
+        rim.wait_send()
+
+    team_bytes(got_sem.at[0]).wait()
+    team_bytes(back_sem.at[0]).wait()
+    for step in range(1, teams):
+        @pl.when(block + step < teams)
+        def _(step=step):
+            forward(step).wait_send()
+
     for out in outs:
         out.wait()
 
@@ -293,14 +370,14 @@
     modes = decay_rate.shape[1]
     groups = channels // LANES
     peers = lax.axis_size("context")
-    chunk = modes * groups // peers
+    teams = peers // modes
     args = (
         streams.transpose(1, 0, 2), short_filter, decay_rate.T, residue.T,
         bias.reshape(groups, LANES),
     )
     hbm = pl.BlockSpec(memory_space=pltpu.HBM)
     table = pltpu.VMEM((modes * groups, LANES), F32)
-    chunks = pltpu.VMEM((peers, chunk, LANES), F32)
+    pieces = pltpu.VMEM((modes, groups, LANES), F32)
     return pl.pallas_call(
         functools.partial(kernel, peers, tokens, groups, modes),
         out_shape=jax.ShapeDtypeStruct((tokens, channels), BF16),
@@ -320,12 +397,18 @@
             table, table, table, table, table,
             pltpu.VMEM((8, channels), F32),
             pltpu.VMEM((8, channels), F32),
-            chunks, chunks, chunks, chunks,
+            pieces,
+            pltpu.VMEM((groups, LANES), F32),
+            pltpu.VMEM((teams - 1, groups, LANES), F32),
+            pieces,
             pltpu.SemaphoreType.DMA((8,)),
             pltpu.SemaphoreType.DMA((groups // 8,)),
             pltpu.SemaphoreType.DMA((2,)),
             pltpu.SemaphoreType.DMA((2,)),
             pltpu.SemaphoreType.DMA((2,)),
+            pltpu.SemaphoreType.DMA((teams - 1,)),
+            pltpu.SemaphoreType.DMA((teams - 1,)),
+            pltpu.SemaphoreType.REGULAR((teams - 1,)),
         ],
         compiler_params=pltpu.CompilerParams(
             collective_id=0, has_side_effects=True, vmem_limit_bytes=40 * 2**20

time: 52.2 us -> 34.1 us (0.65)
  the two profiles are of different devices: /device:TPU:1 before, /device:TPU:481 now
where the time goes in v2:
time: 34.1 us; the launch traced here: 34 us
  Pallas kernels  33 us (97%)
  local copies, waits for them, and re-layouts  0.97 us (3%)
    pallas_call x1, Pallas kernels, body(): pl.pallas_call(functools.partial(kernel, peers, tokens, groups, modes), o...  33 us
    unnamed x1, local copies, waits for them, and re-layouts  0.97 us

profile of v2, /device:TPU:481, one launch (start us, length us, event | category | flops | bytes accessed | tf_op | source)
XLA Modules:
  0.0 34.0 jit_solution(17449240168066716524)
XLA Ops:
  0.0 33.0 %shard_map.55 = bf16[256,2048]{1,0:T(8,128)(2,1)S(1)} custom-call(bf16[3,256,2048]{2,1,0:T(8,128)(2,1)} %bitcast.4, f32[3,3,2048]{2,1,0:T(4,128)} %w_hbm.1, f32[16,2048]{1,0:T(8,128)} %bitcast.5, f32[16,2048]{1,0:T(8,128)} %bitcast.6, f32[16,128]{1,0:T(8,128)} %bitcast.7), custom_call_target="tpu_custom_call" | custom-call | tf_op jit(solution)/shard_map/pallas_call | solution.py:381
  33.0 1.0 %copy.7 = bf16[256,2048]{1,0:T(8,128)(2,1)} copy(bf16[256,2048]{1,0:T(8,128)(2,1)S(1)} %shard_map.55) | data formatting | bytes 2097152

commit v3 on v2

--- a/solution.py
+++ b/solution.py
@@ -28,10 +28,10 @@
 
 def kernel(
     peers, tokens, groups, modes,
-    x_hbm, w_hbm, rate_hbm, res_hbm, bias_hbm, out_hbm,
-    w_ref, rate_ref, res_ref, bias_ref, xv, xt, kvt, yt, qf, ov, rate_cm, pole_cm, res_cm, ends, enter,
+    x_hbm, w_hbm, rate_hbm, res_hbm, bias_hbm, ov,
+    w_ref, rate_ref, res_ref, bias_ref, xv, xt, kvt, yt, qf, rate_cm, pole_cm, res_cm, far_cm, ends, enter,
     rim_out, rim_in, got, total, totals, states_out,
-    load_sem, out_sem, rim_sem, got_sem, back_sem, total_send, total_recv, ready,
+    load_sem, rim_sem, got_sem, back_sem, total_send, total_recv, ready,
 ):
     me = lax.axis_index("context")
     team = modes
@@ -39,7 +39,6 @@
     block, spot = me // team, lax.rem(me, team)
     mine = pl.ds(pl.multiple_of(spot * groups, groups), groups)
     halves = groups // 8
-    wide = 8 * LANES
 
     def at_context(rank):
         return {"device_id": {"context": rank}, "device_id_type": MESH}
@@ -52,8 +51,8 @@
     def greet(rank):
         pl.semaphore_signal(barrier, inc=1, **at_context(rank))
 
-    def greet_mate(step, _):
-        greet(mate(step))
+    def greet_mate(k, _):
+        greet(mate(k))
         return 0
 
     tail = pltpu.make_async_copy(x_hbm.at[:, pl.ds(tokens - 16, 16), :], xt, load_sem.at[3])
@@ -89,6 +88,7 @@
         rate_cm[where, :] = rate
         pole_cm[where, :] = jnp.exp(-rate)
         res_cm[where, :] = res_ref[:, lane]
+        far_cm[where, :] = jnp.exp(rate * (2.0 - tokens))
         return 0
 
     for load in small:
@@ -187,14 +187,13 @@
         lane = pl.ds(pl.multiple_of(g * LANES, LANES), LANES)
         edge = rim_in[:, lane]
         feats = []
-        for i in range(3):
+        for i in (1, 2):
             w = taps(i, lane)
             x = xv[i, pl.ds(0, 16), lane].astype(F32)[0:8]
             before = (pltpu.roll(edge, (8 - 2 * i - 1) % 8, 0), pltpu.roll(edge, (8 - 2 * i) % 8, 0))
             x1, x2, _ = lag_tiles(x, before)
             feats.append(w[0] * x + w[1] * x1 + w[2] * x2)
-        kvt[pl.ds(g, 8, stride=groups), :] = (feats[1] * feats[2]).astype(BF16).astype(F32)
-        qf[pl.ds(0, 8), lane] = feats[0]
+        kvt[pl.ds(g, 8, stride=groups), :] = (feats[0] * feats[1]).astype(BF16).astype(F32)
         return 0
 
     lax.fori_loop(0, groups, first_tile, 0)
@@ -204,12 +203,12 @@
         kv1 = kvt[pl.ds(groups + 8 * h, 8), :]
         for m in range(modes):
             rows = pl.ds(m * groups + 8 * h, 8)
-            far = jnp.exp(rate_cm[rows, :] * (2.0 - tokens))
-            ends[rows, :] = ends[rows, :] + far * (pole_cm[rows, :] * kv0 + kv1)
+            ends[rows, :] = ends[rows, :] + far_cm[rows, :] * (pole_cm[rows, :] * kv0 + kv1)
     def rows_of(to):
         return pl.ds(pl.multiple_of(to * groups, groups), groups)
 
-    def collect(step, _):
+    def collect(k, _):
+        step = k
         pltpu.make_async_remote_copy(
             src_ref=ends.at[rows_of(lax.rem(spot + step, team))], dst_ref=got.at[spot],
             send_sem=got_sem.at[0], recv_sem=got_sem.at[1], **at_context(mate(step)),
@@ -219,8 +218,8 @@
     lax.fori_loop(1, team, collect, 0)
     got[pl.ds(spot, 1), :, :] = ends[mine, :][None]
 
-    def team_bytes(sem):
-        part = got.at[pl.ds(0, team - 1)]
+    def team_bytes(sem, rows=groups):
+        part = got.at[pl.ds(0, team - 1), pl.ds(0, rows)]
         return pltpu.make_async_copy(part, part, sem)
 
     def forward(step):
@@ -260,15 +259,14 @@
         def group(g, _):
             lane = pl.ds(pl.multiple_of(g * LANES, LANES), LANES)
             w = taps(0, lane)
-            zero = jnp.zeros((8, LANES), F32)
-            before = (zero, zero)
+            edge = rim_in[:, lane]
+            before = (pltpu.roll(edge, 7, 0), edge)
             for block in range(tokens // 16):
                 x16 = xv[0, pl.ds(block * 16, 16), lane].astype(F32)
                 for sub in range(2):
                     x = x16[sub * 8:sub * 8 + 8]
                     x1, x2, before = lag_tiles(x, before)
-                    if block or sub:
-                        qf[pl.ds(block * 16 + sub * 8, 8), lane] = w[0] * x + w[1] * x1 + w[2] * x2
+                    qf[pl.ds(block * 16 + sub * 8, 8), lane] = w[0] * x + w[1] * x1 + w[2] * x2
             return 0
 
         lax.fori_loop(0, groups, group, 0)
@@ -297,14 +295,18 @@
         state = state * span + got[j - 1]
         states_out[j, :, :] = state
 
-    def give_back(step, _):
-        pltpu.make_async_remote_copy(
-            src_ref=states_out.at[lax.rem(spot + step, team)], dst_ref=enter.at[mine],
-            send_sem=back_sem.at[0], recv_sem=back_sem.at[1], **at_context(mate(step)),
-        ).start()
-        return 0
-
-    lax.fori_loop(1, team, give_back, 0)
+    for h in range(halves):
+        def give_back(k, _, h=h):
+            step = k
+            cols = pl.ds(8 * h, 8)
+            rows = pl.ds(pl.multiple_of(spot * groups + 8 * h, 8), 8)
+            pltpu.make_async_remote_copy(
+                src_ref=states_out.at[lax.rem(spot + step, team), cols], dst_ref=enter.at[rows],
+                send_sem=back_sem.at[0, h], recv_sem=back_sem.at[1, h], **at_context(mate(step)),
+            ).start()
+            return 0
+
+        lax.fori_loop(1, team, give_back, 0)
     enter[mine, :] = states_out[spot]
     for step in range(2, teams):
         push(step)
@@ -312,16 +314,30 @@
         kept = local_part(h, 0, half, blank)
         kept = local_part(h, half, tokens, kept)
     query_part()
-    team_bytes(back_sem.at[1]).wait()
-
-    outs = []
+    def gate(g, first, count):
+        lane = pl.ds(pl.multiple_of(g * LANES, LANES), LANES)
+        for k in range(count):
+            at = pl.multiple_of((first + k) * 16, 16)
+            mixed = jnp.concatenate(
+                [yt[pl.ds((at + sub) * groups + g, 8, stride=groups), :] for sub in (0, 8)], axis=0
+            )
+            mixed = mixed.astype(BF16).astype(F32)
+            ov[pl.ds(at, 16), lane] = (qf[pl.ds(at, 16), lane] * mixed).astype(BF16)
+
+    steps = tokens // 8
+    per_step = 8 * (tokens // 16) // steps
     for h in range(halves):
+        team_bytes(back_sem.at[1, h], 8).wait()
         poles = vregs(pole_cm, h)
         carried = [
             p * r * s for p, r, s in zip(poles, vregs(res_cm, h), vregs(enter, h))
         ]
 
         def step(i, terms, h=h, poles=poles):
+            if h:
+                blocks = tokens // 16
+                place = i * per_step
+                gate((h - 1) * 8 + place // blocks, lax.rem(place, blocks), per_step)
             for j in range(8):
                 rows = token_rows(i * 8 + j, h)
                 parts = list(terms)
@@ -331,38 +347,25 @@
                 terms = [u * p for u, p in zip(terms, poles)]
             return terms
 
-        lax.fori_loop(0, tokens // 8, step, carried)
-
-        def gate(gi, _, h=h):
-            g = h * 8 + gi
-            lane = pl.ds(pl.multiple_of(g * LANES, LANES), LANES)
-            for block in range(tokens // 16):
-                at = block * 16
-                mixed = jnp.concatenate(
-                    [yt[pl.ds((at + sub) * groups + g, 8, stride=groups), :] for sub in (0, 8)], axis=0
-                )
-                mixed = mixed.astype(BF16).astype(F32)
-                ov[pl.ds(at, 16), lane] = (qf[pl.ds(at, 16), lane] * mixed).astype(BF16)
-            return 0
-
-        lax.fori_loop(0, 8, gate, 0)
-        cols = pl.ds(h * wide, wide)
-        out = pltpu.make_async_copy(ov.at[:, cols], out_hbm.at[:, cols], out_sem.at[h])
-        out.start()
-        outs.append(out)
+        lax.fori_loop(0, steps, step, carried)
+
+    def last_gate(gi, _):
+        gate((halves - 1) * 8 + gi, 0, tokens // 16)
+        return 0
+
+    lax.fori_loop(0, 8, last_gate, 0)
+
     @pl.when(me < peers - 1)
     def _():
         rim.wait_send()
 
     team_bytes(got_sem.at[0]).wait()
-    team_bytes(back_sem.at[0]).wait()
+    for h in range(halves):
+        team_bytes(back_sem.at[0, h], 8).wait()
     for step in range(1, teams):
         @pl.when(block + step < teams)
         def _(step=step):
             forward(step).wait_send()
-
-    for out in outs:
-        out.wait()
 
 
 def body(streams, short_filter, decay_rate, residue, bias):
@@ -382,7 +385,7 @@
         functools.partial(kernel, peers, tokens, groups, modes),
         out_shape=jax.ShapeDtypeStruct((tokens, channels), BF16),
         in_specs=[hbm] * 5,
-        out_specs=pl.BlockSpec(memory_space=pl.ANY),
+        out_specs=pl.BlockSpec(memory_space=pltpu.VMEM),
         scratch_shapes=[
             pltpu.VMEM(short_filter.shape, F32),
             pltpu.VMEM((modes, channels), F32),
@@ -393,8 +396,7 @@
             pltpu.VMEM((tokens * groups, LANES), F32),
             pltpu.VMEM((tokens * groups, LANES), F32),
             pltpu.VMEM((tokens, channels), F32),
-            pltpu.VMEM((tokens, channels), BF16),
-            table, table, table, table, table,
+            table, table, table, table, table, table,
             pltpu.VMEM((8, channels), F32),
             pltpu.VMEM((8, channels), F32),
             pieces,
@@ -402,10 +404,9 @@
             pltpu.VMEM((teams - 1, groups, LANES), F32),
             pieces,
             pltpu.SemaphoreType.DMA((8,)),
-            pltpu.SemaphoreType.DMA((groups // 8,)),
             pltpu.SemaphoreType.DMA((2,)),
             pltpu.SemaphoreType.DMA((2,)),
-            pltpu.SemaphoreType.DMA((2,)),
+            pltpu.SemaphoreType.DMA((2, groups // 8)),
             pltpu.SemaphoreType.DMA((teams - 1,)),
             pltpu.SemaphoreType.DMA((teams - 1,)),
             pltpu.SemaphoreType.REGULAR((teams - 1,)),

time: 34.1 us -> 33.2 us (0.974)
  Pallas kernels: 33 us -> 32.1 us
    pallas_call x1, Pallas kernels: 33 us -> 32.1 us  [body(): pl.pallas_call(functools.partial(kernel, peers, tokens, groups, modes), o...]
where the time goes in v3:
time: 33.2 us; the launch traced here: 33.1 us
  Pallas kernels  32.1 us (97%)
  local copies, waits for them, and re-layouts  0.97 us (3%)
    pallas_call x1, Pallas kernels, body(): pl.pallas_call(functools.partial(kernel, peers, tokens, groups, modes), o...  32.1 us
    unnamed x1, local copies, waits for them, and re-layouts  0.97 us

profile of v3, /device:TPU:481, one launch (start us, length us, event | category | flops | bytes accessed | tf_op | source)
XLA Modules:
  0.0 33.1 jit_solution(10693459020991840027)
XLA Ops:
  0.0 32.1 %shard_map.55 = bf16[256,2048]{1,0:T(8,128)(2,1)S(1)} custom-call(bf16[3,256,2048]{2,1,0:T(8,128)(2,1)} %bitcast.4, f32[3,3,2048]{2,1,0:T(4,128)} %w_hbm.1, f32[16,2048]{1,0:T(8,128)} %bitcast.5, f32[16,2048]{1,0:T(8,128)} %bitcast.6, f32[16,128]{1,0:T(8,128)} %bitcast.7), custom_call_target="tpu_custom_call" | custom-call | tf_op jit(solution)/shard_map/pallas_call | solution.py:384
  32.2 1.0 %copy.7 = bf16[256,2048]{1,0:T(8,128)(2,1)} copy(bf16[256,2048]{1,0:T(8,128)(2,1)S(1)} %shard_map.55) | data formatting | bytes 2097152

commit v4 on v3

--- a/solution.py
+++ b/solution.py
@@ -338,6 +338,9 @@
                 blocks = tokens // 16
                 place = i * per_step
                 gate((h - 1) * 8 + place // blocks, lax.rem(place, blocks), per_step)
+            if h == halves - 1:
+                for q in range(4):
+                    gate(h * 8 + lax.rem(i, 2) * 4 + q, jnp.maximum(i // 2 - 1, 0), 1)
             for j in range(8):
                 rows = token_rows(i * 8 + j, h)
                 parts = list(terms)
@@ -350,7 +353,7 @@
         lax.fori_loop(0, steps, step, carried)
 
     def last_gate(gi, _):
-        gate((halves - 1) * 8 + gi, 0, tokens // 16)
+        gate((halves - 1) * 8 + gi, tokens // 16 - 1, 1)
         return 0
 
     lax.fori_loop(0, 8, last_gate, 0)

time: 33.2 us -> 33 us (level)
  no operation moved by 1% of the time
where the time goes in v4:
time: 33 us; the launch traced here: 32.9 us
  Pallas kernels  31.9 us (97%)
  local copies, waits for them, and re-layouts  0.97 us (3%)
    pallas_call x1, Pallas kernels, body(): pl.pallas_call(functools.partial(kernel, peers, tokens, groups, modes), o...  31.9 us
    unnamed x1, local copies, waits for them, and re-layouts  0.97 us

profile of v4, /device:TPU:481, one launch (start us, length us, event | category | flops | bytes accessed | tf_op | source)
XLA Modules:
  0.0 32.9 jit_solution(17569931943226784562)
XLA Ops:
  0.0 31.9 %shard_map.55 = bf16[256,2048]{1,0:T(8,128)(2,1)S(1)} custom-call(bf16[3,256,2048]{2,1,0:T(8,128)(2,1)} %bitcast.4, f32[3,3,2048]{2,1,0:T(4,128)} %w_hbm.1, f32[16,2048]{1,0:T(8,128)} %bitcast.5, f32[16,2048]{1,0:T(8,128)} %bitcast.6, f32[16,128]{1,0:T(8,128)} %bitcast.7), custom_call_target="tpu_custom_call" | custom-call | tf_op jit(solution)/shard_map/pallas_call | solution.py:387
  31.9 1.0 %copy.7 = bf16[256,2048]{1,0:T(8,128)(2,1)} copy(bf16[256,2048]{1,0:T(8,128)(2,1)S(1)} %shard_map.55) | data formatting | bytes 2097152
